TPU v7x, 256 devices: a whole 4x4x8 slice. The times are simulated.
256 devices in a mesh: side: 2 (over y_hi), row: 8 (over z), col: 16 (over x, y_lo, core).
Axes of the slice: x: 4, y: 4 (y_hi: 2, y_lo: 2; y = y_hi * 2 + y_lo), z: 8, core: 2. Of those that a mesh axis runs over, the one named last changes fastest.
Arguments:
- queries: bfloat16 [512, 8192], P(('row', 'col')), may hold values from -4.5 to 16
- new_entries: bfloat16 [512, 2048], P(('row', 'col')), may hold values from -4.5 to 15.875
- cache_keys: bfloat16 [2, 512, 256, 1024], P('side', ('row', 'col')), may hold values from -4.5 to 16
- cache_values: bfloat16 [2, 512, 256, 1024], P('side', ('row', 'col')), may hold values from -6 to 6
- lengths: int32 [512], P(('row', 'col')), may hold values from 1 to 256, 32768 in all
- residual: bfloat16 [512, 8192], P(None, 'col'), may hold values from -16 to 16
- norm_gain: bfloat16 [8192], P('col'), may hold values from 0.099609375 to 1.8984375
- out_weight: bfloat16 [2, 8192, 8192], P('side', 'row', 'col'), may hold values from -0.125 to 0.125
- gate_weight: bfloat16 [2, 8192, 14336], P('side', 'col', 'row'), may hold values from -0.0625 to 0.0625
- up_weight: bfloat16 [2, 8192, 14336], P('side', 'col', 'row'), may hold values from -0.0625 to 0.0625
- down_weight: bfloat16 [2, 14336, 8192], P('side', 'row', 'col'), may hold values from -0.046875 to 0.046875
Outputs:
- layer_out: bfloat16 [512, 8192], P(('row', 'col'), 'side')
All inputs are finite; a program needn't handle non-finite values. No bound on the sum of `lengths` on one device may be relied on, other than what follows from the above.
Results may differ from a plain program's by a relative error of at most 0.025.
Values may be sent and summed in bfloat16 or wider, within the bound.
No kernel may reach another device: no remote copies, remote signals or barrier semaphores. Data moves between devices by JAX's collectives and lax.ppermute only.
A program may use at most 64 MiB of HBM per device.

v0:
```python
import jax
import jax.numpy as jnp
from jax import lax
from jax.sharding import PartitionSpec as P

D = 8192
H = 64
KVH = 8
HD = 128
ORIG = 64
rope_theta = 500000.0
stretch_factor = 8.0
eps = 1e-05


def from_behind(value, axis, steps):
    count = lax.axis_size(axis)
    first, last = (max(0, -steps), min(count, count - steps))
    return lax.ppermute(value, axis, [(source, source + steps) for source in range(first, last)])


def frequencies(lengths):
    seq = lengths.astype(jnp.float32) + 1.0
    stretch = jnp.maximum(stretch_factor * seq / ORIG - (stretch_factor - 1.0), 1.0)
    log_base = jnp.log(jnp.float32(rope_theta)) + HD / (HD - 2.0) * jnp.log(stretch)
    expo = jnp.arange(HD // 2).astype(jnp.float32) * (2.0 / HD)
    return jnp.exp(-expo[None, :] * log_base[:, None])


def rotary(vec, angles):
    half = vec.shape[-1] // 2
    first = vec[..., :half]
    second = vec[..., half:]
    cosine = jnp.cos(angles)
    sine = jnp.sin(angles)
    return jnp.concatenate(
        [first * cosine - second * sine, second * cosine + first * sine], axis=-1
    )


def attention(queries, new_entries, keys, values, lengths):
    slots = queries.shape[0]
    span = keys.shape[1]
    per_group = H // KVH
    freqs = frequencies(lengths)
    angle_new = lengths.astype(jnp.float32)[:, None] * freqs
    angle_cache = jnp.arange(span).astype(jnp.float32)[None, :, None] * freqs[:, None, :]
    query_rot = rotary(
        queries.astype(jnp.float32).reshape(slots, H, HD), angle_new[:, None, :]
    ).astype(jnp.bfloat16)
    query_rot = query_rot.reshape(slots, KVH, per_group, HD)
    key_fresh = new_entries[:, : KVH * HD].astype(jnp.float32).reshape(slots, KVH, HD)
    value_fresh = new_entries[:, KVH * HD :].astype(jnp.float32).reshape(slots, KVH, HD)
    key_new_rot = rotary(key_fresh, angle_new[:, None, :]).astype(jnp.bfloat16)
    key_rot = rotary(
        keys.astype(jnp.float32).reshape(slots, span, KVH, HD), angle_cache[:, :, None, :]
    ).astype(jnp.bfloat16)
    scale = HD ** (-0.5)
    scores = (
        jnp.einsum("sgqd,scgd->sgqc", query_rot, key_rot, preferred_element_type=jnp.float32)
        * scale
    )
    own_score = (
        jnp.einsum("sgqd,sgd->sgq", query_rot, key_new_rot, preferred_element_type=jnp.float32)
        * scale
    )
    valid_mask = (jnp.arange(span)[None, :] < lengths[:, None])[:, None, None, :]
    highest = jnp.maximum(jnp.max(jnp.where(valid_mask, scores, -1e30), axis=-1), own_score)
    weights = jnp.where(valid_mask, jnp.exp(scores - highest[..., None]), 0.0)
    own_weight = jnp.exp(own_score - highest)
    totals = jnp.sum(weights, axis=-1) + own_weight
    weights16 = weights.astype(jnp.bfloat16)
    mixed = jnp.einsum(
        "sgqc,scgd->sgqd",
        weights16,
        values.reshape(slots, span, KVH, HD),
        preferred_element_type=jnp.float32,
    )
    mixed = mixed + own_weight[..., None] * value_fresh[:, :, None, :]
    return (mixed / totals[..., None]).reshape(slots, H * HD).astype(jnp.bfloat16)


def local(
    queries,
    new_entries,
    cache_keys,
    cache_values,
    lengths,
    residual,
    norm_gain,
    out_weight,
    gate_weight,
    up_weight,
    down_weight,
):
    attended = attention(queries, new_entries, cache_keys[0], cache_values[0], lengths)
    slot_count = attended.shape[0]
    row_count = lax.axis_size("row")
    col_count = lax.axis_size("col")
    head_block = attended.shape[1] // row_count
    split_heads = attended.reshape(slot_count, row_count, head_block)
    moved = from_behind(split_heads, "side", 1)
    blocks = lax.all_to_all(moved, "row", split_axis=1, concat_axis=0, tiled=True)
    sectioned = blocks.reshape(row_count, 1, slot_count, head_block)
    out_block = out_weight[0]
    partial_value = jnp.einsum(
        "akjd,de->akje",
        lax.all_gather(sectioned, "col", axis=1, tiled=True),
        out_block,
        preferred_element_type=jnp.float32,
    )
    col_width = out_block.shape[1]
    total_rows = row_count * col_count * slot_count
    projected = lax.psum(
        partial_value.reshape(total_rows, col_width).astype(jnp.bfloat16), "row"
    ).astype(jnp.float32)
    stream = residual.astype(jnp.float32) + projected
    squares = lax.psum(jnp.sum(stream * stream, axis=1), "col")
    inv_rms = lax.rsqrt(squares / D + eps)
    normed = (stream * inv_rms[:, None] * norm_gain.astype(jnp.float32)[None, :]).astype(
        jnp.bfloat16
    )
    gate_block = gate_weight[0]
    up_block = up_weight[0]
    down_block = down_weight[0]
    gate_part = jnp.dot(normed, gate_block, preferred_element_type=jnp.float32)
    up_part = jnp.dot(normed, up_block, preferred_element_type=jnp.float32)
    gate_total, up_total = (
        lax.psum(gate_part.astype(jnp.bfloat16), "col").astype(jnp.float32),
        lax.psum(up_part.astype(jnp.bfloat16), "col").astype(jnp.float32),
    )
    hidden = (jax.nn.silu(gate_total) * up_total).astype(jnp.bfloat16)
    down_part = jnp.dot(hidden, down_block, preferred_element_type=jnp.float32)
    down_total = lax.psum(down_part.astype(jnp.bfloat16), "row").astype(jnp.float32)
    final = (stream + down_total).astype(jnp.bfloat16)
    group_rows = col_count * slot_count
    mine_rows = lax.dynamic_slice_in_dim(final, lax.axis_index("row") * group_rows, group_rows, 0)
    slot_rows = lax.all_to_all(mine_rows, "col", split_axis=0, concat_axis=1, tiled=True)
    half_width = slot_rows.shape[1] // 2
    returned = from_behind(slot_rows[:, :half_width], "side", -1)
    return jnp.where(lax.axis_index("side") == 0, returned, slot_rows[:, half_width:])


def solution(mesh):
    in_specs = (
        P(("row", "col"), None),
        P(("row", "col"), None),
        P("side", ("row", "col"), None, None),
        P("side", ("row", "col"), None, None),
        P(("row", "col")),
        P(None, "col"),
        P("col"),
        P("side", "row", "col"),
        P("side", "col", "row"),
        P("side", "col", "row"),
        P("side", "row", "col"),
    )
    out_specs = P(("row", "col"), "side")
    return jax.shard_map(local, mesh=mesh, in_specs=in_specs, out_specs=out_specs, check_vma=False)
```

profile of v0, /device:TPU:1, one launch (start us, length us, event | category | flops | bytes accessed | tf_op | source)
XLA Modules:
  0.0 439.4 jit_solution(3323142169381161737)
XLA Ops:
  6.5 0.8 convert_element_type.82
  7.3 0.7 multiply_add_fusion
  8.0 0.7 iota_compare_fusion
  8.7 3.9 copy.23
  12.7 4.2 fusion.50
  16.8 3.8 copy.32
  20.6 3.8 copy.33
  24.5 0.1 multiply_cosine_fusion.1
  24.7 0.1 fusion.41
  24.8 0.1 subtract_convert_fusion.2
  24.9 1.9 multiply_cosine_fusion
  26.7 0.1 maximum_bitcast_fusion
  26.8 0.2 fusion.43
  27.1 4.7 %subtract_convert_fusion = (bf16[4,256,8,64]{3,1,2,0:T(8,128)(2,1)S(1)}, bf16[4,256,8,64]{3,1,2,0:T(8,128)(2,1)S(1)}) fusion(f32[4,256,8,64]{3,1,2,0:T(8,128)} %copy.33, f32[4,256,8,64]{3,1,2,0:T(8,128)} %copy.32, f32[4,256,64]{2,1,0:T(8,128)S(1)} %get-tuple-element.22, f32[4,256,64]{2,1,0:T(8,128)S(1)} %get-tuple-element.21), kind=kLoop, calls=%fused_computation.3 | loop fusion | flops 4194304 | bytes 6815744 | tf_op jit(solution)/shard_map/convert.6
  31.8 1.3 select_reduce_fusion
  33.2 0.2 fusion.34
  33.4 0.6 copy.36
  34.0 0.4 fusion.30
  34.5 0.1 copy.27
  34.6 5.7 %collective-permute-start = (bf16[4,8,1024]{2,0,1:T(4,128)(2,1)S(1)}, bf16[4,8,1024]{2,0,1:T(4,128)(2,1)S(1)}, u32[]{:S(2)}, u32[]{:S(2)}) collective-permute-start(bf16[4,8,1024]{2,0,1:T(4,128)(2,1)S(1)} %copy.27), channel_id=1, source_target_pairs={{0,128},{1,129},{2,130},{3,131},{4,132},{5,133},{6,134},{7,135},{8... | collective-permute-start | bytes 196616 | tf_op jit(solution)/shard_map/ppermute | solution.py:19
  40.3 1.3 collective-permute-done
  41.6 15.3 %all_to_all.34 = bf16[4,8,1024]{2,0,1:T(4,128)(2,1)S(1)} all-to-all(bf16[4,8,1024]{2,0,1:T(4,128)(2,1)S(1)} %collective-permute-done), channel_id=1, replica_groups=mesh['side'=2,'row'=8,'col'=16] {'row'}, dimensions={1} | all-to-all | bytes 131072 | tf_op jit(solution)/shard_map/all_to_all | solution.py:103
  56.9 0.6 copy.28
  57.5 0.0 all-gather.3.cloned.1.call-update
  57.5 0.0 all-reduce.5.cloned.1.call-start
  57.6 34.6 %all-gather.3.cloned.1.call-done = bf16[8,64,1,1024]{3,0,2,1:T(8,128)(2,1)} async-done(((bf16[8,4,1,1024]{3,0,2,1:T(8,128)(2,1)}), bf16[8,64,1,1024]{3,0,2,1:T(8,128)(2,1)}) %all-gather.3.cloned.1.call-update) | async-done | bytes 1048592 | tf_op jit(solution)/shard_map/all_gather | solution.py:108
  92.2 1.8 copy.29
  94.0 0.0 copy-start.6
  94.1 2.8 convolution_convert_fusion.2
  96.9 0.0 all-reduce.5.cloned.1.call-update
  96.9 0.0 all-reduce.9.cloned.1.call-start
  96.9 68.6 %all-reduce.5.cloned.1.call-done = bf16[512,512]{1,0:T(8,128)(2,1)} async-done(((bf16[512,512]{1,0:T(8,128)(2,1)}), bf16[512,512]{1,0:T(8,128)(2,1)}) %all-reduce.5.cloned.1.call-update) | async-done | bytes 524304 | tf_op jit(solution)/shard_map/psum | solution.py:114
  165.5 1.3 multiply_reduce_fusion
  166.8 31.7 %psum.36 = f32[512]{0:T(512)S(1)} all-reduce(f32[512]{0:T(512)S(1)} %get-tuple-element.13), channel_id=1, replica_groups=mesh['side'=2,'row'=8,'col'=16] {'col'}, use_global_device_ids=true, to_apply=%region_4.5 | all-reduce | flops 512 | bytes 4096 | tf_op jit(solution)/shard_map/psum | solution.py:118
  198.6 0.0 copy-start.7
  198.6 3.6 convolution_convert_fusion.1
  202.2 2.5 convolution_convert_fusion
  204.7 0.0 all-reduce.9.cloned.1.call-update
  204.7 0.0 all-reduce.7.cloned.1.call-start
  204.8 129.6 %all-reduce.9.cloned.1.call-done = (bf16[512,1792]{1,0:T(8,128)(2,1)}, bf16[512,1792]{1,0:T(8,128)(2,1)}) async-done(((bf16[512,1792]{1,0:T(8,128)(2,1)}, bf16[512,1792]{1,0:T(8,128)(2,1)}), (bf16[512,1792]{1,0:T(8,128)(2,1)}, bf16[512,1792]{1,0:T(8,128)(2,1)})) %all-reduce.9.cloned.1.call-update) | async-done | bytes 3670032 | tf_op jit(solution)/shard_map/psum | solution.py:130
  334.4 4.6 %fusion.16 = bf16[512,512]{1,0:T(8,128)(2,1)} fusion(bf16[1,1792,512]{2,1,0:T(8,128)(2,1)} %param.21, bf16[512,1792]{1,0:T(8,128)(2,1)} %get-tuple-element.5, bf16[512,1792]{1,0:T(8,128)(2,1)} %get-tuple-element.6), kind=kOutput, calls=%fused_computation.21 | convolution fusion | flops 947126272 | bytes 6029312 | tf_op jit(solution)/shard_map/dot_general | solution.py:133
  339.0 0.0 all-reduce.7.cloned.1.call-update
  339.0 70.0 %all-reduce.7.cloned.1.call-done = bf16[512,512]{1,0:T(8,128)(2,1)} async-done(((bf16[512,512]{1,0:T(8,128)(2,1)}), bf16[512,512]{1,0:T(8,128)(2,1)}) %all-reduce.7.cloned.1.call-update) | async-done | bytes 524304 | tf_op jit(solution)/shard_map/psum | solution.py:134
  409.1 0.9 fusion.37
  409.9 16.1 %all_to_all.35 = bf16[16,4,512]{2,1,0:T(4,128)(2,1)S(1)} all-to-all(bf16[16,4,512]{2,1,0:T(4,128)(2,1)S(1)} %all_to_all.28), channel_id=1, replica_groups=mesh['side'=2,'row'=8,'col'=16] {'col'}, dimensions={0} | all-to-all | bytes 131072 | tf_op jit(solution)/shard_map/all_to_all | solution.py:138
  426.0 1.3 collective-permute-start.1
  427.3 4.9 %collective-permute-done.1 = bf16[4,4096]{1,0:T(4,128)(2,1)S(1)} collective-permute-done((bf16[4,4096]{1,0:T(4,128)(2,1)S(1)}, bf16[4,4096]{1,0:T(4,128)(2,1)S(1)}, u32[]{:S(2)}, u32[]{:S(2)}) %collective-permute-start.1) | collective-permute-done | bytes 32800 | tf_op jit(solution)/shard_map/ppermute | solution.py:19
  432.2 0.6 slice_select_fusion
  (28 shorter events, 0.2 us)
Async XLA Ops:
  6.5 192.0 %copy-start = (bf16[1,512,1792]{2,1,0:T(8,128)(2,1)S(1)}, bf16[1,512,1792]{2,1,0:T(8,128)(2,1)}, u32[]{:S(2)}) copy-start(bf16[1,512,1792]{2,1,0:T(8,128)(2,1)} %param.19) | copy-start | bytes 5505028
  6.5 85.7 %all-gather.3.cloned.1.call-start = ((), (), s32[]{:S(2)}) async-start(), calls=%async_computation.4 | async-start | bytes 1114112 | tf_op jit(solution)/shard_map/all_gather | solution.py:108
  20.6 3.8 copy-start.4
  20.6 3.9 copy-start.5
  31.8 1.6 copy-start.1
  34.6 7.0 %collective-permute-start = (bf16[4,8,1024]{2,0,1:T(4,128)(2,1)S(1)}, bf16[4,8,1024]{2,0,1:T(4,128)(2,1)S(1)}, u32[]{:S(2)}, u32[]{:S(2)}) collective-permute-start(bf16[4,8,1024]{2,0,1:T(4,128)(2,1)S(1)} %copy.27), channel_id=1, source_target_pairs={{0,128},{1,129},{2,130},{3,131},{4,132},{5,133},{6,134},{7,135},{8... | collective-permute-start | bytes 196616 | tf_op jit(solution)/shard_map/ppermute | solution.py:19
  57.5 108.0 %all-reduce.5.cloned.1.call-start = ((), (), s32[]{:S(2)}) async-start(), calls=%async_computation.2 | async-start | bytes 1048576 | tf_op jit(solution)/shard_map/psum | solution.py:114
  94.0 2.9 copy-start.6
  94.0 71.5 %copy-start.2 = (bf16[512,512]{1,0:T(8,128)(2,1)S(1)}, bf16[512,512]{1,0:T(8,128)(2,1)}, u32[]{:S(2)}) copy-start(bf16[512,512]{1,0:T(8,128)(2,1)} %param.16) | copy-start | bytes 1572868
  96.9 237.5 %all-reduce.9.cloned.1.call-start = ((), (), s32[]{:S(2)}) async-start(), calls=%async_computation.5 | async-start | bytes 7340032 | tf_op jit(solution)/shard_map/psum | solution.py:130
  198.6 3.7 copy-start.3
  198.6 3.7 copy-start.7
  204.7 204.3 %all-reduce.7.cloned.1.call-start = ((), (), s32[]{:S(2)}) async-start(), calls=%async_computation.3 | async-start | bytes 1048576 | tf_op jit(solution)/shard_map/psum | solution.py:134
  426.0 6.2 %collective-permute-start.1 = (bf16[4,4096]{1,0:T(4,128)(2,1)S(1)}, bf16[4,4096]{1,0:T(4,128)(2,1)S(1)}, u32[]{:S(2)}, u32[]{:S(2)}) collective-permute-start(bf16[4,4096]{1,0:T(4,128)(2,1)S(1)} %slice.46), channel_id=1, source_target_pairs={{128,0},{129,1},{130,2},{131,3},{132,4},{133,5},{134,6},{135,7},{1... | collective-permute-start | bytes 98312 | tf_op jit(solution)/shard_map/ppermute | solution.py:19
Sparse Core Ops, SparseCore 0:
  57.7 34.5 all-gather.2
  97.0 68.4 all-reduce.4
  204.8 129.5 all-reduce.8
  339.1 69.8 all-reduce.6
where the time goes:
time: 440 us; the launch traced here: 439 us
  waiting for transfers between devices  309 us (70%)
  blocking collectives  63.1 us (14%)
  local copies, waits for them, and re-layouts  19 us (4%)
  matrix products  15.5 us (4%)
  between operations  13.3 us (3%)
  other arithmetic  12.2 us (3%)
  starting transfers between devices  7.07 us (2%)
    psum x1, waiting for transfers between devices, local(): lax.psum(up_part.astype(jnp.bfloat16), 'col').astype(jnp.float32)  130 us
    psum x1, waiting for transfers between devices, local(): lax.psum(down_part.astype(jnp.bfloat16), 'row').astype(jnp.float32)  70 us
    psum x1, waiting for transfers between devices, local(): lax.psum(partial_value.reshape(total_rows, col_width).astype(jnp.bfloat16...  68.6 us
    all_gather x1, waiting for transfers between devices, local(): lax.all_gather(sectioned, 'col', axis=1, tiled=True)  34.6 us
    psum x1, blocking collectives, local(): squares = lax.psum(jnp.sum(stream * stream, axis=1), 'col')  31.7 us
    all_to_all x1, blocking collectives, local(): lax.all_to_all(mine_rows, 'col', split_axis=0, concat_axis=1, tiled=True)  16.1 us
    all_to_all x1, blocking collectives, local(): lax.all_to_all(moved, 'row', split_axis=1, concat_axis=0, tiled=True)  15.3 us
    unnamed x21, local copies, waits for them, and re-layouts  12.2 us
  transfers between devices with their start and end apart: 6, of which 6 were waited for; matrix products, arithmetic and copies ran while one was open for 0% of the time, Pallas kernels for 0%

commit v1 on v0

--- a/solution.py
+++ b/solution.py
@@ -135,7 +135,10 @@
     final = (stream + down_total).astype(jnp.bfloat16)
     group_rows = col_count * slot_count
     mine_rows = lax.dynamic_slice_in_dim(final, lax.axis_index("row") * group_rows, group_rows, 0)
-    slot_rows = lax.all_to_all(mine_rows, "col", split_axis=0, concat_axis=1, tiled=True)
+    slot_rows = jnp.concatenate(
+        lax.all_to_all(jnp.stack(jnp.split(mine_rows, lax.axis_size("col"), axis=0)), "col", 0, 0),
+        axis=1,
+    )
     half_width = slot_rows.shape[1] // 2
     returned = from_behind(slot_rows[:, :half_width], "side", -1)
     return jnp.where(lax.axis_index("side") == 0, returned, slot_rows[:, half_width:])

time: 440 us -> 440 us (level)
    unnamed x21 -> x36, local copies, waits for them, and re-layouts: 12.2 us -> 12.4 us
where the time goes in v1:
time: 440 us
  waiting for transfers between devices  309 us (70%)
  blocking collectives  63.1 us (14%)
  local copies, waits for them, and re-layouts  19.1 us (4%)
  matrix products  15.5 us (4%)
  between operations  13.4 us (3%)
  other arithmetic  12.2 us (3%)
  starting transfers between devices  7.07 us (2%)
    psum x1, waiting for transfers between devices, local(): lax.psum(up_part.astype(jnp.bfloat16), 'col').astype(jnp.float32)  130 us
    psum x1, waiting for transfers between devices, local(): lax.psum(down_part.astype(jnp.bfloat16), 'row').astype(jnp.float32)  70 us
    psum x1, waiting for transfers between devices, local(): lax.psum(partial_value.reshape(total_rows, col_width).astype(jnp.bfloat16...  68.6 us
    all_gather x1, waiting for transfers between devices, local(): lax.all_gather(sectioned, 'col', axis=1, tiled=True)  34.6 us
    psum x1, blocking collectives, local(): squares = lax.psum(jnp.sum(stream * stream, axis=1), 'col')  31.7 us
    all_to_all x1, blocking collectives, local(): lax.all_to_all(jnp.stack(jnp.split(mine_rows, lax.axis_size('col'), axis=...  16.1 us
    all_to_all x1, blocking collectives, local(): lax.all_to_all(moved, 'row', split_axis=1, concat_axis=0, tiled=True)  15.3 us
    unnamed x36, local copies, waits for them, and re-layouts  12.4 us
  transfers between devices with their start and end apart: 6, of which 6 were waited for; matrix products, arithmetic and copies ran while one was open for 0% of the time, Pallas kernels for 0%

profile of v1, /device:TPU:1, one launch (start us, length us, event | category | flops | bytes accessed | tf_op | source)
XLA Modules:
  0.0 439.6 jit_solution(7047048930196050104)
XLA Ops:
  6.5 0.8 convert_element_type.82
  7.3 0.7 multiply_add_fusion
  8.0 0.7 iota_compare_fusion
  8.7 3.9 copy.23
  12.7 4.2 fusion.50
  16.8 3.8 copy.32
  20.6 3.8 copy.33
  24.5 0.1 multiply_cosine_fusion.1
  24.7 0.1 fusion.41
  24.8 0.1 subtract_convert_fusion.2
  24.9 1.9 multiply_cosine_fusion
  26.7 0.1 maximum_bitcast_fusion
  26.8 0.2 fusion.43
  27.1 4.7 %subtract_convert_fusion = (bf16[4,256,8,64]{3,1,2,0:T(8,128)(2,1)S(1)}, bf16[4,256,8,64]{3,1,2,0:T(8,128)(2,1)S(1)}) fusion(f32[4,256,8,64]{3,1,2,0:T(8,128)} %copy.33, f32[4,256,8,64]{3,1,2,0:T(8,128)} %copy.32, f32[4,256,64]{2,1,0:T(8,128)S(1)} %get-tuple-element.22, f32[4,256,64]{2,1,0:T(8,128)S(1)} %get-tuple-element.21), kind=kLoop, calls=%fused_computation.3 | loop fusion | flops 4194304 | bytes 6815744 | tf_op jit(solution)/shard_map/convert.6
  31.8 1.3 select_reduce_fusion
  33.2 0.2 fusion.34
  33.4 0.6 copy.36
  34.0 0.4 fusion.30
  34.5 0.1 copy.27
  34.6 5.7 %collective-permute-start = (bf16[4,8,1024]{2,0,1:T(4,128)(2,1)S(1)}, bf16[4,8,1024]{2,0,1:T(4,128)(2,1)S(1)}, u32[]{:S(2)}, u32[]{:S(2)}) collective-permute-start(bf16[4,8,1024]{2,0,1:T(4,128)(2,1)S(1)} %copy.27), channel_id=1, source_target_pairs={{0,128},{1,129},{2,130},{3,131},{4,132},{5,133},{6,134},{7,135},{8... | collective-permute-start | bytes 196616 | tf_op jit(solution)/shard_map/ppermute | solution.py:19
  40.3 1.3 collective-permute-done
  41.6 15.3 %all_to_all.20 = bf16[4,8,1024]{2,0,1:T(4,128)(2,1)S(1)} all-to-all(bf16[4,8,1024]{2,0,1:T(4,128)(2,1)S(1)} %collective-permute-done), channel_id=1, replica_groups=mesh['side'=2,'row'=8,'col'=16] {'row'}, dimensions={1} | all-to-all | bytes 131072 | tf_op jit(solution)/shard_map/all_to_all | solution.py:103
  56.9 0.6 copy.28
  57.5 0.0 all-gather.3.cloned.1.call-update
  57.5 0.0 all-reduce.5.cloned.1.call-start
  57.6 34.6 %all-gather.3.cloned.1.call-done = bf16[8,64,1,1024]{3,0,2,1:T(8,128)(2,1)} async-done(((bf16[8,4,1,1024]{3,0,2,1:T(8,128)(2,1)}), bf16[8,64,1,1024]{3,0,2,1:T(8,128)(2,1)}) %all-gather.3.cloned.1.call-update) | async-done | bytes 1048592 | tf_op jit(solution)/shard_map/all_gather | solution.py:108
  92.2 1.8 copy.29
  94.0 0.0 copy-start.6
  94.1 2.8 convolution_convert_fusion.2
  96.9 0.0 all-reduce.5.cloned.1.call-update
  96.9 0.0 all-reduce.9.cloned.1.call-start
  96.9 68.6 %all-reduce.5.cloned.1.call-done = bf16[512,512]{1,0:T(8,128)(2,1)} async-done(((bf16[512,512]{1,0:T(8,128)(2,1)}), bf16[512,512]{1,0:T(8,128)(2,1)}) %all-reduce.5.cloned.1.call-update) | async-done | bytes 524304 | tf_op jit(solution)/shard_map/psum | solution.py:114
  165.5 1.3 multiply_reduce_fusion
  166.8 31.7 %psum.36 = f32[512]{0:T(512)S(1)} all-reduce(f32[512]{0:T(512)S(1)} %get-tuple-element.13), channel_id=1, replica_groups=mesh['side'=2,'row'=8,'col'=16] {'col'}, use_global_device_ids=true, to_apply=%region_4.5 | all-reduce | flops 512 | bytes 4096 | tf_op jit(solution)/shard_map/psum | solution.py:118
  198.6 0.0 copy-start.7
  198.6 3.6 convolution_convert_fusion.1
  202.2 2.5 convolution_convert_fusion
  204.7 0.0 all-reduce.9.cloned.1.call-update
  204.7 0.0 all-reduce.7.cloned.1.call-start
  204.8 129.6 %all-reduce.9.cloned.1.call-done = (bf16[512,1792]{1,0:T(8,128)(2,1)}, bf16[512,1792]{1,0:T(8,128)(2,1)}) async-done(((bf16[512,1792]{1,0:T(8,128)(2,1)}, bf16[512,1792]{1,0:T(8,128)(2,1)}), (bf16[512,1792]{1,0:T(8,128)(2,1)}, bf16[512,1792]{1,0:T(8,128)(2,1)})) %all-reduce.9.cloned.1.call-update) | async-done | bytes 3670032 | tf_op jit(solution)/shard_map/psum | solution.py:130
  334.4 4.6 %fusion.16 = bf16[512,512]{1,0:T(8,128)(2,1)} fusion(bf16[1,1792,512]{2,1,0:T(8,128)(2,1)} %param.21, bf16[512,1792]{1,0:T(8,128)(2,1)} %get-tuple-element.5, bf16[512,1792]{1,0:T(8,128)(2,1)} %get-tuple-element.6), kind=kOutput, calls=%fused_computation.21 | convolution fusion | flops 947126272 | bytes 6029312 | tf_op jit(solution)/shard_map/dot_general | solution.py:133
  339.0 0.0 all-reduce.7.cloned.1.call-update
  339.0 70.0 %all-reduce.7.cloned.1.call-done = bf16[512,512]{1,0:T(8,128)(2,1)} async-done(((bf16[512,512]{1,0:T(8,128)(2,1)}), bf16[512,512]{1,0:T(8,128)(2,1)}) %all-reduce.7.cloned.1.call-update) | async-done | bytes 524304 | tf_op jit(solution)/shard_map/psum | solution.py:134
  409.1 0.9 fusion.37
  410.1 16.1 %all_to_all.21 = bf16[16,4,512]{2,1,0:T(4,128)(2,1)S(1)} all-to-all(bf16[16,4,512]{2,1,0:T(4,128)(2,1)S(1)} %constant_dynamic-update-slice_fusion), channel_id=1, replica_groups=mesh['side'=2,'row'=8,'col'=16] {'col'}, dimensions={0} | all-to-all | bytes 131072 | tf_op jit(solution)/shard_map/all_to_all | solution.py:139
  426.2 1.3 collective-permute-start.1
  427.5 4.9 %collective-permute-done.1 = bf16[4,4096]{1,0:T(4,128)(2,1)S(1)} collective-permute-done((bf16[4,4096]{1,0:T(4,128)(2,1)S(1)}, bf16[4,4096]{1,0:T(4,128)(2,1)S(1)}, u32[]{:S(2)}, u32[]{:S(2)}) %collective-permute-start.1) | collective-permute-done | bytes 32800 | tf_op jit(solution)/shard_map/ppermute | solution.py:19
  432.4 0.6 slice_select_fusion
  (43 shorter events, 0.4 us)
Async XLA Ops:
  6.5 192.0 %copy-start = (bf16[1,512,1792]{2,1,0:T(8,128)(2,1)S(1)}, bf16[1,512,1792]{2,1,0:T(8,128)(2,1)}, u32[]{:S(2)}) copy-start(bf16[1,512,1792]{2,1,0:T(8,128)(2,1)} %param.19) | copy-start | bytes 5505028
  6.5 85.7 %all-gather.3.cloned.1.call-start = ((), (), s32[]{:S(2)}) async-start(), calls=%async_computation.4 | async-start | bytes 1114112 | tf_op jit(solution)/shard_map/all_gather | solution.py:108
  20.6 3.8 copy-start.4
  20.6 3.9 copy-start.5
  31.8 1.6 copy-start.1
  34.6 7.0 %collective-permute-start = (bf16[4,8,1024]{2,0,1:T(4,128)(2,1)S(1)}, bf16[4,8,1024]{2,0,1:T(4,128)(2,1)S(1)}, u32[]{:S(2)}, u32[]{:S(2)}) collective-permute-start(bf16[4,8,1024]{2,0,1:T(4,128)(2,1)S(1)} %copy.27), channel_id=1, source_target_pairs={{0,128},{1,129},{2,130},{3,131},{4,132},{5,133},{6,134},{7,135},{8... | collective-permute-start | bytes 196616 | tf_op jit(solution)/shard_map/ppermute | solution.py:19
  57.5 108.0 %all-reduce.5.cloned.1.call-start = ((), (), s32[]{:S(2)}) async-start(), calls=%async_computation.2 | async-start | bytes 1048576 | tf_op jit(solution)/shard_map/psum | solution.py:114
  94.0 2.9 copy-start.6
  94.0 71.5 %copy-start.2 = (bf16[512,512]{1,0:T(8,128)(2,1)S(1)}, bf16[512,512]{1,0:T(8,128)(2,1)}, u32[]{:S(2)}) copy-start(bf16[512,512]{1,0:T(8,128)(2,1)} %param.16) | copy-start | bytes 1572868
  96.9 237.5 %all-reduce.9.cloned.1.call-start = ((), (), s32[]{:S(2)}) async-start(), calls=%async_computation.5 | async-start | bytes 7340032 | tf_op jit(solution)/shard_map/psum | solution.py:130
  198.6 3.7 copy-start.3
  198.6 3.7 copy-start.7
  204.7 204.3 %all-reduce.7.cloned.1.call-start = ((), (), s32[]{:S(2)}) async-start(), calls=%async_computation.3 | async-start | bytes 1048576 | tf_op jit(solution)/shard_map/psum | solution.py:134
  426.2 6.2 %collective-permute-start.1 = (bf16[4,4096]{1,0:T(4,128)(2,1)S(1)}, bf16[4,4096]{1,0:T(4,128)(2,1)S(1)}, u32[]{:S(2)}, u32[]{:S(2)}) collective-permute-start(bf16[4,4096]{1,0:T(4,128)(2,1)S(1)} %slice.46), channel_id=1, source_target_pairs={{128,0},{129,1},{130,2},{131,3},{132,4},{133,5},{134,6},{135,7},{1... | collective-permute-start | bytes 98312 | tf_op jit(solution)/shard_map/ppermute | solution.py:19
Sparse Core Ops, SparseCore 0:
  57.7 34.5 all-gather.2
  97.0 68.4 all-reduce.4
  204.8 129.5 all-reduce.8
  339.1 69.8 all-reduce.6
